TPU v7x, 128 devices: a whole 4x4x4 slice. The times are simulated.
128 devices in a mesh: freq: 8 (over z, x_hi), rcv: 16 (over x_lo, y, core).
Axes of the slice: x: 4 (x_hi: 2, x_lo: 2; x = x_hi * 2 + x_lo), y: 4, z: 4, core: 2. Of those that a mesh axis runs over, the one named last changes fastest.
Arguments:
- reflection: float32 [128, 2, 1024, 2048], P('freq', None, None, 'rcv'), may hold values from -0.09375 to 0.09375
- focusing_input: float32 [128, 2, 32, 2048], P('freq', None, None, 'rcv'), may hold values from -6 to 6
- direct_wave: float32 [256, 32, 2048], P(None, 'freq', 'rcv'), may hold values from -6 to 6
- mute_source: int32 [32, 1024], P('rcv', 'freq'), may hold values from 32 to 127
- mute_receiver: int32 [32, 2048], P('freq', 'rcv'), may hold values from 32 to 127
Outputs:
- focus_minus: float32 [256, 32, 1024], P(None, 'rcv', 'freq')
- focus_plus: float32 [256, 32, 2048], P(None, 'freq', 'rcv')
All inputs are finite; a program needn't handle non-finite values.
Results may differ from a plain program's by a relative error of at most 0.00007.
Values sent between devices are 32-bit elements; how exact they have to be, the bound alone decides.
No kernel may reach another device: no remote copies, remote signals or barrier semaphores. Data moves between devices by JAX's collectives and lax.ppermute only.
A program may use at most 128 MiB of HBM per device.

v0:
```python
import math
import jax
import jax.numpy as jnp
from jax import lax
from jax.sharding import PartitionSpec as P

MAXIMUM_ACCURACY = lax.Precision.HIGHEST


def dft_tables(freqs, samples):
    index_freq = lax.broadcasted_iota(jnp.int32, (freqs, samples), 0) + 1
    index_time = lax.broadcasted_iota(jnp.int32, (freqs, samples), 1)
    phase_turns = jnp.mod(index_freq * index_time, samples).astype(jnp.float32) * (
        2.0 * math.pi / samples
    )
    return (jnp.cos(phase_turns), jnp.sin(phase_turns))


def window(traces, mute_table):
    samples = traces.shape[0]
    time_index = lax.broadcasted_iota(jnp.int32, (samples, 1, 1), 0)
    kept_mask = (time_index < mute_table[None]) | (time_index > samples - mute_table[None])
    return jnp.where(kept_mask, traces, jnp.zeros_like(traces))


def forward_panel(reflection, focusing_input):
    reflection_real = reflection[:, 0]
    reflection_imaginary = reflection[:, 1]
    real_part = jnp.einsum(
        "ual,uel->eua", reflection_real, focusing_input[:, 0], precision=MAXIMUM_ACCURACY
    ) - jnp.einsum(
        "ual,uel->eua", reflection_imaginary, focusing_input[:, 1], precision=MAXIMUM_ACCURACY
    )
    imag_part = jnp.einsum(
        "ual,uel->eua", reflection_real, focusing_input[:, 1], precision=MAXIMUM_ACCURACY
    ) + jnp.einsum(
        "ual,uel->eua", reflection_imaginary, focusing_input[:, 0], precision=MAXIMUM_ACCURACY
    )
    return jnp.stack((real_part, imag_part), axis=2)


def adjoint_panel(reflection, receiver_panel):
    reflection_real = reflection[:, 0]
    reflection_imaginary = reflection[:, 1]
    real_part = jnp.einsum(
        "klh,lhc->klc", receiver_panel[:, :, 0], reflection_real, precision=MAXIMUM_ACCURACY
    ) + jnp.einsum(
        "klh,lhc->klc", receiver_panel[:, :, 1], reflection_imaginary, precision=MAXIMUM_ACCURACY
    )
    imag_part = jnp.einsum(
        "klh,lhc->klc", receiver_panel[:, :, 1], reflection_real, precision=MAXIMUM_ACCURACY
    ) - jnp.einsum(
        "klh,lhc->klc", receiver_panel[:, :, 0], reflection_imaginary, precision=MAXIMUM_ACCURACY
    )
    return jnp.stack((real_part, imag_part), axis=2)


def to_time(spectrum, cosine, sine_table, factor):
    return factor * (
        jnp.einsum("akb,kt->tab", spectrum[:, :, 0], cosine, precision=MAXIMUM_ACCURACY)
        - jnp.einsum("akb,kt->tab", spectrum[:, :, 1], sine_table, precision=MAXIMUM_ACCURACY)
    )


def to_freq(traces, cosine, sine_table, factor):
    real_part = factor * jnp.einsum("tab,kt->akb", traces, cosine, precision=MAXIMUM_ACCURACY)
    imag_part = -factor * jnp.einsum("tab,kt->akb", traces, sine_table, precision=MAXIMUM_ACCURACY)
    return jnp.stack((real_part, imag_part), axis=2)


def body(reflection, focusing_input, direct_wave, mute_source, mute_receiver):
    freqs = reflection.shape[0] * lax.axis_size("freq")
    samples = 2 * freqs
    factor = 1.0 / math.sqrt(freqs)
    cosine, sine_table = dft_tables(freqs, samples)
    share = mute_source.shape[0]
    term = forward_panel(reflection, focusing_input)
    summed = lax.psum(term, "rcv")
    spectrum = lax.all_to_all(summed, "freq", split_axis=3, concat_axis=1, tiled=True)
    mutes_all = lax.all_gather(mute_source, "rcv", axis=0, tiled=True)
    windowed = window(to_time(spectrum, cosine, sine_table, factor), mutes_all)
    focus_minus = lax.dynamic_slice_in_dim(windowed, lax.axis_index("rcv") * share, share, 1)
    back_local = to_freq(windowed, cosine, sine_table, factor)
    back_spec = lax.all_to_all(back_local, "freq", split_axis=1, concat_axis=3, tiled=True)
    adjoint = adjoint_panel(reflection, back_spec)
    receiver_spec = lax.all_to_all(adjoint, "freq", split_axis=0, concat_axis=1, tiled=True)
    adj_time = to_time(receiver_spec, cosine, sine_table, factor)
    focus_plus = direct_wave - window(adj_time, mute_receiver)
    return (focus_minus, focus_plus)


def solution(mesh):
    placed = (
        P("freq", None, None, "rcv"),
        P("freq", None, None, "rcv"),
        P(None, "freq", "rcv"),
        P("rcv", "freq"),
        P("freq", "rcv"),
    )
    return jax.shard_map(
        body,
        mesh=mesh,
        in_specs=placed,
        out_specs=(P(None, "rcv", "freq"), P(None, "freq", "rcv")),
        check_vma=False,
    )
```

profile of v0, /device:TPU:0, one launch (start us, length us, event | category | flops | bytes accessed | tf_op | source)
XLA Modules:
  0.0 455.7 jit_solution(1087763690156176081)
XLA Ops:
  7.2 10.8 %fusion.4 = f32[16,32,1024]{2,1,0:T(8,128)S(1)} fusion(f32[16,2,1024,128]{3,2,1,0:T(8,128)} %param.5, f32[16,2,32,128]{3,2,1,0:T(8,128)} %param.6), kind=kOutput, calls=%fused_computation.4 | convolution fusion | flops 805306368 | bytes 10747904 | tf_op jit(solution)/shard_map/ual,uel->eua/dot_general | solution.py:36
  18.1 11.1 %fusion.6 = f32[16,32,1024]{2,1,0:T(8,128)S(1)} fusion(f32[16,2,1024,128]{3,2,1,0:T(8,128)} %param.5, f32[16,2,32,128]{3,2,1,0:T(8,128)S(1)} %copy-done.4), kind=kOutput, calls=%fused_computation.6 | convolution fusion | flops 805306368 | bytes 10747904 | tf_op jit(solution)/shard_map/ual,uel->eua/dot_general | solution.py:31
  29.2 8.4 %add_bitcast_fusion = f32[32,16,1,1024]{3,0,1,2:T(8,128)S(1)} fusion(f32[16,32,1024]{2,1,0:T(8,128)S(1)} %fusion.4, f32[16,2,1024,128]{3,2,1,0:T(8,128)S(1)} %copy-done, f32[16,2,32,128]{3,2,1,0:T(8,128)S(1)} %copy-done.4), kind=kOutput, calls=%fused_computation.38 | convolution fusion | flops 805830656 | bytes 12845056 | tf_op jit(solution)/shard_map/ual,uel->eua/dot_general | solution.py:34
  37.6 8.6 %subtract_bitcast_fusion = f32[32,16,1,1024]{3,0,1,2:T(8,128)S(1)} fusion(f32[16,32,1024]{2,1,0:T(8,128)S(1)} %fusion.6, f32[16,2,1024,128]{3,2,1,0:T(8,128)S(1)} %copy-done, f32[16,2,32,128]{3,2,1,0:T(8,128)S(1)} %copy-done.4), kind=kOutput, calls=%fused_computation.39 | convolution fusion | flops 805830656 | bytes 12845056 | tf_op jit(solution)/shard_map/ual,uel->eua/dot_general | solution.py:29
  48.8 132.0 %all-reduce.2.cloned.1.call-done = f32[32,16,2,1024]{3,0,1,2:T(8,128)} async-done(((f32[32,16,2,1024]{3,0,1,2:T(8,128)}), f32[32,16,2,1024]{3,0,1,2:T(8,128)}) %all-reduce.2.cloned.1.call-update) | async-done | bytes 4194320 | tf_op jit(solution)/shard_map/psum | solution.py:78
  180.8 14.3 %copy.23 = f32[32,16,2,1024]{0,1,2,3:T(8,128)} copy(f32[32,16,2,1024]{3,0,1,2:T(8,128)} %all-reduce.2.cloned.1.call-done) | data formatting | bytes 8388608 | tf_op jit(solution)/shard_map/psum | solution.py:78
  195.1 12.8 %reshape.16 = f32[8,1,131072]{2,1,0:T(1,128)} reshape(f32[1024,2,16,32]{3,2,1,0:T(8,128)} %bitcast.140) | data formatting | bytes 8388608
  207.9 6.7 %all-to-all-start = ((f32[8,1,131072]{2,1,0:T(1,128)}), f32[8,1,131072]{2,1,0:T(1,128)}, u32[]{:S(2)}, u32[]{:S(2)}) async-start(f32[8,1,131072]{2,1,0:T(1,128)} %reshape.16), calls=%async_computation | async-start | bytes 8388608 | tf_op jit(solution)/shard_map/all_to_all | solution.py:79
  214.6 58.8 %all-gather = s32[16,2,128]{2,1,0:T(2,128)S(1)} all-gather(s32[1,2,128]{2,1,0:T(2,128)S(1)} %bitcast.151), channel_id=1, replica_groups=mesh['freq'=8,'rcv'=16] {'rcv'}, dimensions={0}, use_global_device_ids=true | all-gather | bytes 17408 | tf_op jit(solution)/shard_map/all_gather | solution.py:80
  274.0 13.7 %reduce = f32[8,131072]{1,0:T(8,128)} reduce(f32[8,1,131072]{2,1,0:T(1,128)} %all-to-all-done, f32[]{:T(128)} %broadcast.42), dimensions={1}, to_apply=%all_to_all.39.reduce_sub_computation | reduce | bytes 8388612 | tf_op jit(solution)/shard_map/all_to_all | solution.py:79
  287.7 13.4 %reshape.17 = f32[1024,2,16,32]{3,2,1,0:T(8,128)} reshape(f32[8,131072]{1,0:T(8,128)} %reduce) | data formatting | bytes 8388608
  301.0 13.5 %copy.24 = f32[32,16,2,8,128]{4,1,3,0,2:T(8,128)} copy(f32[32,16,2,8,128]{0,1,2,4,3:T(8,128)} %bitcast.141) | data formatting | bytes 8388608 | tf_op jit(solution)/shard_map/all_to_all | solution.py:79
  314.6 5.8 %fusion.25 = f32[256,32,128]{2,0,1:T(8,128)S(1)} fusion(f32[32,128,2,128]{3,1,0,2:T(8,128)} %bitcast.142, s32[128]{0:T(128)S(1)} %iota_add_fusion), kind=kOutput, calls=%fused_computation.35 | convolution fusion | flops 1611071488 | bytes 6291968 | tf_op jit(solution)/shard_map/akb,kt->tab/dot_general | solution.py:60
  320.4 5.0 %multiply_select_fusion = f32[256,32,128]{2,0,1:T(8,128)S(1)} fusion(f32[256,32,128]{2,0,1:T(8,128)S(1)} %fusion.25, f32[32,128,2,128]{3,1,0,2:T(8,128)S(1)} %bitcast.143, s32[32,128]{1,0:T(8,128)S(1)} %broadcast_subtract_fusion, s32[32,128]{1,0:T(8,128)S(1)} %bitcast.150, s32[128]{0:T(128)S(1)} %iota_add_fusion), kind=kOutput, calls=%fused_computation.27 | convolution fusion | flops 1617362944 | bytes 10519040 | tf_op jit(solution)/shard_map/akb,kt->tab/dot_general | solution.py:61
  328.2 3.0 multiply_bitcast_fusion.1
  334.2 58.4 %all_to_all.54 = f32[32,128,2,128]{3,0,2,1:T(8,128)S(1)} all-to-all(f32[32,128,2,128]{3,0,2,1:T(8,128)S(1)} %copy.27), channel_id=1, replica_groups=mesh['freq'=8,'rcv'=16] {'freq'}, dimensions={1} | all-to-all | bytes 8388608 | tf_op jit(solution)/shard_map/all_to_all | solution.py:84
  392.6 5.8 %copy.44 = f32[32,8,16,2,128]{4,1,0,2,3:T(8,128)} copy(f32[32,8,16,2,128]{4,0,3,2,1:T(8,128)S(1)} %bitcast.144) | data formatting | bytes 8388608 | tf_op jit(solution)/shard_map/all_to_all | solution.py:84
  398.4 4.9 %all_to_all.46 = f32[32,16,2,1024]{3,0,1,2:T(8,128)} reshape(f32[32,16,2,8,128]{4,3,0,1,2:T(8,128)} %bitcast.145) | data formatting | bytes 8388608 | tf_op jit(solution)/shard_map/all_to_all | solution.py:84
  403.3 7.3 %fusion = f32[16,32,128]{2,1,0:T(8,128)S(1)} fusion(f32[16,2,1024,128]{3,2,1,0:T(8,128)} %param.5, f32[32,16,2,1024]{3,0,1,2:T(8,128)} %all_to_all.46), kind=kOutput, calls=%fused_computation | convolution fusion | flops 805306368 | bytes 10747904 | tf_op jit(solution)/shard_map/klh,lhc->klc/dot_general | solution.py:52
  410.6 7.3 %fusion.2 = f32[16,32,128]{2,1,0:T(8,128)S(1)} fusion(f32[16,2,1024,128]{3,2,1,0:T(8,128)} %param.5, f32[32,16,2,1024]{3,0,1,2:T(8,128)} %all_to_all.46), kind=kOutput, calls=%fused_computation.2 | convolution fusion | flops 805306368 | bytes 10747904 | tf_op jit(solution)/shard_map/klh,lhc->klc/dot_general | solution.py:47
  417.9 7.2 %fusion.42 = f32[32,16,1,128]{3,0,1,2:T(8,128)S(1)} fusion(f32[16,32,128]{2,1,0:T(8,128)S(1)} %fusion, f32[16,2,1024,128]{3,2,1,0:T(8,128)} %param.5, f32[32,16,2,1024]{3,0,1,2:T(8,128)S(1)} %copy-done.2), kind=kOutput, calls=%fused_computation.47 | convolution fusion | flops 805371904 | bytes 11010048 | tf_op jit(solution)/shard_map/klh,lhc->klc/dot_general | solution.py:50
  425.1 4.5 fusion.36
  430.7 3.5 all-to-all-start.2
  436.1 9.0 %all-to-all-done.2 = f32[32,16,2,128]{3,1,2,0:T(8,128)S(1)} async-done(((f32[32,16,2,128]{3,1,2,0:T(8,128)}), f32[32,16,2,128]{3,1,2,0:T(8,128)S(1)}, u32[]{:S(2)}, u32[]{:S(2)}) %all-to-all-start.2) | async-done | bytes 524320 | tf_op jit(solution)/shard_map/all_to_all | solution.py:86
  (44 shorter events, 15.4 us)
Async XLA Ops:
  7.2 10.9 %copy-start.4 = (f32[16,2,32,128]{3,2,1,0:T(8,128)S(1)}, f32[16,2,32,128]{3,2,1,0:T(8,128)}, u32[]{:S(2)}) copy-start(f32[16,2,32,128]{3,2,1,0:T(8,128)} %param.6) | copy-start | bytes 1572868
  7.2 173.6 %all-reduce.2.cloned.1.call-start = ((), (), s32[]{:S(2)}) async-start(), calls=%async_computation.3 | async-start | bytes 8388608 | tf_op jit(solution)/shard_map/psum | solution.py:78
  7.2 22.0 %copy-start = (f32[16,2,1024,128]{3,2,1,0:T(8,128)S(1)}, f32[16,2,1024,128]{3,2,1,0:T(8,128)}, u32[]{:S(2)}) copy-start(f32[16,2,1024,128]{3,2,1,0:T(8,128)} %param.5) | copy-start | bytes 50331652
  207.9 6.7 %copy-start.7 = (s32[2,128]{1,0:T(2,128)S(1)}, s32[2,128]{1,0:T(2,128)}, u32[]{:S(2)}) copy-start(s32[2,128]{1,0:T(2,128)} %param.8) | copy-start | bytes 3076
  207.9 65.5 %all-to-all-start = ((f32[8,1,131072]{2,1,0:T(1,128)}), f32[8,1,131072]{2,1,0:T(1,128)}, u32[]{:S(2)}, u32[]{:S(2)}) async-start(f32[8,1,131072]{2,1,0:T(1,128)} %reshape.16), calls=%async_computation | async-start | bytes 8388608 | tf_op jit(solution)/shard_map/all_to_all | solution.py:79
  314.6 5.8 %copy-start.3 = (f32[32,16,2,8,128]{4,1,3,0,2:T(8,128)S(1)}, f32[32,16,2,8,128]{4,1,3,0,2:T(8,128)}, u32[]{:S(2)}) copy-start(f32[32,16,2,8,128]{4,1,3,0,2:T(8,128)} %copy.24) | copy-start | bytes 12582916
  325.4 2.9 copy-start.1
  403.3 21.8 %slice-start = ((s8[16777216]{0:T(1024)(128)(4,1)}), s8[4194304]{0:T(1024)(128)(4,1)S(1)}, s32[]{:S(2)}) async-start(s8[16777216]{0:T(1024)(128)(4,1)} %bitcast.138), calls=%async_computation.4 | async-start | bytes 8388608
  403.3 21.8 %slice-start.1 = ((s8[16777216]{0:T(1024)(128)(4,1)}), s8[4194304]{0:T(1024)(128)(4,1)S(1)}, s32[]{:S(2)}) async-start(s8[16777216]{0:T(1024)(128)(4,1)} %bitcast.138), calls=%async_computation.5 | async-start | bytes 8388608
  410.6 7.3 %copy-start.2 = (f32[32,16,2,1024]{3,0,1,2:T(8,128)S(1)}, f32[32,16,2,1024]{3,0,1,2:T(8,128)}, u32[]{:S(2)}) copy-start(f32[32,16,2,1024]{3,0,1,2:T(8,128)} %all_to_all.46) | copy-start | bytes 12582916
  410.6 14.5 %slice-start.2 = ((s8[16777216]{0:T(1024)(128)(4,1)}), s8[4194304]{0:T(1024)(128)(4,1)S(1)}, s32[]{:S(2)}) async-start(s8[16777216]{0:T(1024)(128)(4,1)} %bitcast.138), calls=%async_computation.6 | async-start | bytes 8388608
  417.9 7.2 %slice-start.3 = ((s8[16777216]{0:T(1024)(128)(4,1)}), s8[4194304]{0:T(1024)(128)(4,1)S(1)}, s32[]{:S(2)}) async-start(s8[16777216]{0:T(1024)(128)(4,1)} %bitcast.138), calls=%async_computation.7 | async-start | bytes 8388608
  425.1 9.2 %copy-start.6 = (s32[4,128]{1,0:T(4,128)S(1)}, s32[4,128]{1,0:T(4,128)}, u32[]{:S(2)}) copy-start(s32[4,128]{1,0:T(4,128)} %param.9) | copy-start | bytes 6148
  429.6 16.6 %copy-start.5 = (f32[256,4,128]{2,1,0:T(4,128)S(1)}, f32[256,4,128]{2,1,0:T(4,128)}, u32[]{:S(2)}) copy-start(f32[256,4,128]{2,1,0:T(4,128)} %param.7) | copy-start | bytes 1572868
  430.7 14.4 %all-to-all-start.2 = ((f32[32,16,2,128]{3,1,2,0:T(8,128)}), f32[32,16,2,128]{3,1,2,0:T(8,128)S(1)}, u32[]{:S(2)}, u32[]{:S(2)}) async-start(f32[32,16,2,128]{3,1,2,0:T(8,128)} %copy.29), calls=%async_computation.2 | async-start | bytes 1048576 | tf_op jit(solution)/shard_map/all_to_all | solution.py:86
Sparse Core Ops, SparseCore 0:
  48.9 131.7 all-reduce.1
where the time goes:
time: 462 us; the launch traced here: 456 us
  waiting for transfers between devices  141 us (31%)
  blocking collectives  117 us (25%)
  matrix products  84 us (18%)
  local copies, waits for them, and re-layouts  71.9 us (16%)
  other arithmetic  16.8 us (4%)
  between operations  14.6 us (3%)
  starting transfers between devices  10.2 us (2%)
    psum x1, waiting for transfers between devices, body(): summed = lax.psum(term, 'rcv')  132 us
    all_gather x1, blocking collectives, body(): mutes_all = lax.all_gather(mute_source, 'rcv', axis=0, tiled=True)  58.8 us
    all_to_all x1, blocking collectives, body(): lax.all_to_all(back_local, 'freq', split_axis=1, concat_axis=3, tiled=True)  58.4 us
    unnamed x28, local copies, waits for them, and re-layouts  28.3 us
    psum x1, local copies, waits for them, and re-layouts, body(): summed = lax.psum(term, 'rcv')  14.3 us
    all_to_all x2, local copies, waits for them, and re-layouts, body(): lax.all_to_all(summed, 'freq', split_axis=3, concat_axis=1, tiled=True)  14 us
    all_to_all x1, other arithmetic, body(): lax.all_to_all(summed, 'freq', split_axis=3, concat_axis=1, tiled=True)  13.7 us
    dot_general x1, matrix products, forward_panel(): jnp.einsum('ual,uel->eua', reflection_imaginary, focusing_input[:, 1], pr...  11.1 us
  transfers between devices with their start and end apart: 3, of which 2 were waited for; matrix products, arithmetic and copies ran while one was open for 0% of the time, Pallas kernels for 0%

commit v1 on v0

--- a/solution.py
+++ b/solution.py
@@ -75,7 +75,8 @@
     cosine, sine_table = dft_tables(freqs, samples)
     share = mute_source.shape[0]
     term = forward_panel(reflection, focusing_input)
-    summed = lax.psum(term, "rcv")
+    y_new = lax.all_gather(term, "rcv")
+    summed = jnp.sum(y_new, 0)
     spectrum = lax.all_to_all(summed, "freq", split_axis=3, concat_axis=1, tiled=True)
     mutes_all = lax.all_gather(mute_source, "rcv", axis=0, tiled=True)
     windowed = window(to_time(spectrum, cosine, sine_table, factor), mutes_all)

time: 462 us -> 685 us (1.48)
  waiting for transfers between devices: 141 us -> 340 us
  other arithmetic: 16.8 us -> 39.8 us
    all_gather x0 -> x1, waiting for transfers between devices: none -> 331 us  [body(): y_new = lax.all_gather(term, 'rcv')]
    psum x1 -> x0, waiting for transfers between devices: 132 us -> none  [body(): summed = lax.psum(term, 'rcv')]
    reduce_sum x0 -> x1, other arithmetic: none -> 23 us  [body(): summed = jnp.sum(y_new, 0)]
    psum x1 -> x0, local copies, waits for them, and re-layouts: 14.3 us -> none  [body(): summed = lax.psum(term, 'rcv')]
    reduce_sum x0 -> x1, local copies, waits for them, and re-layouts: none -> 14.3 us  [body(): summed = jnp.sum(y_new, 0)]
where the time goes in v1:
time: 685 us; the launch traced here: 679 us
  waiting for transfers between devices  340 us (50%)
  blocking collectives  118 us (17%)
  matrix products  84 us (12%)
  local copies, waits for them, and re-layouts  71.9 us (10%)
  other arithmetic  39.8 us (6%)
  between operations  14.6 us (2%)
  starting transfers between devices  10.5 us (2%)
    all_gather x1, waiting for transfers between devices, body(): y_new = lax.all_gather(term, 'rcv')  331 us
    all_gather x1, blocking collectives, body(): mutes_all = lax.all_gather(mute_source, 'rcv', axis=0, tiled=True)  60 us
    all_to_all x1, blocking collectives, body(): lax.all_to_all(back_local, 'freq', split_axis=1, concat_axis=3, tiled=True)  58.4 us
    unnamed x28, local copies, waits for them, and re-layouts  28.3 us
    reduce_sum x1, other arithmetic, body(): summed = jnp.sum(y_new, 0)  23 us
    reduce_sum x1, local copies, waits for them, and re-layouts, body(): summed = jnp.sum(y_new, 0)  14.3 us
    all_to_all x2, local copies, waits for them, and re-layouts, body(): lax.all_to_all(summed, 'freq', split_axis=3, concat_axis=1, tiled=True)  14 us
  transfers between devices with their start and end apart: 3, of which 2 were waited for; matrix products, arithmetic and copies ran while one was open for 0% of the time, Pallas kernels for 0%

profile of v1, /device:TPU:0, one launch (start us, length us, event | category | flops | bytes accessed | tf_op | source)
XLA Modules:
  0.0 679.4 jit_solution(10258308595810735700)
XLA Ops:
  7.2 10.8 %fusion.4 = f32[16,32,1024]{2,1,0:T(8,128)S(1)} fusion(f32[16,2,1024,128]{3,2,1,0:T(8,128)} %param.5, f32[16,2,32,128]{3,2,1,0:T(8,128)} %param.6), kind=kOutput, calls=%fused_computation.4 | convolution fusion | flops 805306368 | bytes 10747904 | tf_op jit(solution)/shard_map/ual,uel->eua/dot_general | solution.py:36
  18.1 11.1 %fusion.6 = f32[16,32,1024]{2,1,0:T(8,128)S(1)} fusion(f32[16,2,1024,128]{3,2,1,0:T(8,128)} %param.5, f32[16,2,32,128]{3,2,1,0:T(8,128)S(1)} %copy-done.4), kind=kOutput, calls=%fused_computation.6 | convolution fusion | flops 805306368 | bytes 10747904 | tf_op jit(solution)/shard_map/ual,uel->eua/dot_general | solution.py:31
  29.2 8.4 %add_bitcast_fusion = f32[32,16,1,1024]{3,0,1,2:T(8,128)S(1)} fusion(f32[16,32,1024]{2,1,0:T(8,128)S(1)} %fusion.4, f32[16,2,1024,128]{3,2,1,0:T(8,128)S(1)} %copy-done, f32[16,2,32,128]{3,2,1,0:T(8,128)S(1)} %copy-done.4), kind=kOutput, calls=%fused_computation.38 | convolution fusion | flops 805830656 | bytes 12845056 | tf_op jit(solution)/shard_map/ual,uel->eua/dot_general | solution.py:34
  37.6 8.6 %subtract_bitcast_fusion = f32[32,16,1,1024]{3,0,1,2:T(8,128)S(1)} fusion(f32[16,32,1024]{2,1,0:T(8,128)S(1)} %fusion.6, f32[16,2,1024,128]{3,2,1,0:T(8,128)S(1)} %copy-done, f32[16,2,32,128]{3,2,1,0:T(8,128)S(1)} %copy-done.4), kind=kOutput, calls=%fused_computation.39 | convolution fusion | flops 805830656 | bytes 12845056 | tf_op jit(solution)/shard_map/ual,uel->eua/dot_general | solution.py:29
  48.8 331.2 %all-gather.4.cloned.1.call-done = f32[512,16,2,1024]{3,0,1,2:T(8,128)} async-done(((f32[32,16,2,1024]{3,0,1,2:T(8,128)}), f32[512,16,2,1024]{3,0,1,2:T(8,128)}) %all-gather.4.cloned.1.call-update) | async-done | bytes 67108880 | tf_op jit(solution)/shard_map/all_gather | solution.py:78
  380.1 23.0 %reduce_sum.9 = f32[32,16,2,1024]{3,0,1,2:T(8,128)} reduce(f32[16,32,16,2,1024]{4,1,0,2,3:T(8,128)} %bitcast.11, f32[]{:T(128)} %constant.16.clone.1), dimensions={0}, to_apply=%region_0.1 | reduce | flops 15728640 | bytes 71303168 | tf_op jit(solution)/shard_map/reduce_sum | solution.py:79
  403.1 14.3 %copy.50 = f32[32,16,2,1024]{0,1,2,3:T(8,128)} copy(f32[32,16,2,1024]{3,0,1,2:T(8,128)} %reduce_sum.9) | data formatting | bytes 8388608 | tf_op jit(solution)/shard_map/reduce_sum | solution.py:79
  417.4 12.8 %reshape.17 = f32[8,1,131072]{2,1,0:T(1,128)} reshape(f32[1024,2,16,32]{3,2,1,0:T(8,128)} %bitcast.142) | data formatting | bytes 8388608
  430.2 7.0 %all-to-all-start = ((f32[8,1,131072]{2,1,0:T(1,128)}), f32[8,1,131072]{2,1,0:T(1,128)}, u32[]{:S(2)}, u32[]{:S(2)}) async-start(f32[8,1,131072]{2,1,0:T(1,128)} %reshape.17), calls=%async_computation | async-start | bytes 8388608 | tf_op jit(solution)/shard_map/all_to_all | solution.py:80
  437.2 60.0 %all-gather.1 = s32[16,2,128]{2,1,0:T(2,128)S(1)} all-gather(s32[1,2,128]{2,1,0:T(2,128)S(1)} %bitcast.153), channel_id=1, replica_groups=mesh['freq'=8,'rcv'=16] {'rcv'}, dimensions={0}, use_global_device_ids=true | all-gather | bytes 17408 | tf_op jit(solution)/shard_map/all_gather | solution.py:81
  497.7 13.7 %reduce = f32[8,131072]{1,0:T(8,128)} reduce(f32[8,1,131072]{2,1,0:T(1,128)} %all-to-all-done, f32[]{:T(128)} %broadcast.42), dimensions={1}, to_apply=%all_to_all.39.reduce_sub_computation | reduce | bytes 8388612 | tf_op jit(solution)/shard_map/all_to_all | solution.py:80
  511.4 13.4 %reshape.18 = f32[1024,2,16,32]{3,2,1,0:T(8,128)} reshape(f32[8,131072]{1,0:T(8,128)} %reduce) | data formatting | bytes 8388608
  524.8 13.5 %copy.52 = f32[32,8,16,2,128]{4,2,1,0,3:T(8,128)} copy(f32[32,8,16,2,128]{0,2,3,4,1:T(8,128)} %bitcast.143) | data formatting | bytes 8388608 | tf_op jit(solution)/shard_map/all_to_all | solution.py:80
  538.3 5.8 fusion.25
  544.1 5.0 multiply_select_fusion
  557.9 58.4 %all_to_all.54 = f32[32,128,2,128]{3,0,2,1:T(8,128)S(1)} all-to-all(f32[32,128,2,128]{3,0,2,1:T(8,128)S(1)} %copy.55), channel_id=1, replica_groups=mesh['freq'=8,'rcv'=16] {'freq'}, dimensions={1} | all-to-all | bytes 8388608 | tf_op jit(solution)/shard_map/all_to_all | solution.py:85
  616.3 5.8 copy.74
  622.1 4.9 all_to_all.46
  627.0 7.3 %fusion = f32[16,32,128]{2,1,0:T(8,128)S(1)} fusion(f32[16,2,1024,128]{3,2,1,0:T(8,128)} %param.5, f32[32,16,2,1024]{3,0,1,2:T(8,128)} %all_to_all.46), kind=kOutput, calls=%fused_computation | convolution fusion | flops 805306368 | bytes 10747904 | tf_op jit(solution)/shard_map/klh,lhc->klc/dot_general | solution.py:52
  634.3 7.3 %fusion.2 = f32[16,32,128]{2,1,0:T(8,128)S(1)} fusion(f32[16,2,1024,128]{3,2,1,0:T(8,128)} %param.5, f32[32,16,2,1024]{3,0,1,2:T(8,128)} %all_to_all.46), kind=kOutput, calls=%fused_computation.2 | convolution fusion | flops 805306368 | bytes 10747904 | tf_op jit(solution)/shard_map/klh,lhc->klc/dot_general | solution.py:47
  641.6 7.2 %fusion.42 = f32[32,16,1,128]{3,0,1,2:T(8,128)S(1)} fusion(f32[16,32,128]{2,1,0:T(8,128)S(1)} %fusion, f32[16,2,1024,128]{3,2,1,0:T(8,128)} %param.5, f32[32,16,2,1024]{3,0,1,2:T(8,128)S(1)} %copy-done.2), kind=kOutput, calls=%fused_computation.47 | convolution fusion | flops 805371904 | bytes 11010048 | tf_op jit(solution)/shard_map/klh,lhc->klc/dot_general | solution.py:50
  648.8 4.5 fusion.36
  654.5 3.5 all-to-all-start.2
  659.9 8.9 %all-to-all-done.2 = f32[32,16,2,128]{3,1,2,0:T(8,128)S(1)} async-done(((f32[32,16,2,128]{3,1,2,0:T(8,128)}), f32[32,16,2,128]{3,1,2,0:T(8,128)S(1)}, u32[]{:S(2)}, u32[]{:S(2)}) %all-to-all-start.2) | async-done | bytes 524320 | tf_op jit(solution)/shard_map/all_to_all | solution.py:87
  (45 shorter events, 18.5 us)
Async XLA Ops:
  7.2 10.9 %copy-start.4 = (f32[16,2,32,128]{3,2,1,0:T(8,128)S(1)}, f32[16,2,32,128]{3,2,1,0:T(8,128)}, u32[]{:S(2)}) copy-start(f32[16,2,32,128]{3,2,1,0:T(8,128)} %param.6) | copy-start | bytes 1572868
  7.2 372.9 %all-gather.4.cloned.1.call-start = ((), (), s32[]{:S(2)}) async-start(), calls=%async_computation.3 | async-start | bytes 71303168 | tf_op jit(solution)/shard_map/all_gather | solution.py:78
  7.2 22.0 %copy-start = (f32[16,2,1024,128]{3,2,1,0:T(8,128)S(1)}, f32[16,2,1024,128]{3,2,1,0:T(8,128)}, u32[]{:S(2)}) copy-start(f32[16,2,1024,128]{3,2,1,0:T(8,128)} %param.5) | copy-start | bytes 50331652
  430.2 7.0 %copy-start.7 = (s32[2,128]{1,0:T(2,128)S(1)}, s32[2,128]{1,0:T(2,128)}, u32[]{:S(2)}) copy-start(s32[2,128]{1,0:T(2,128)} %param.8) | copy-start | bytes 3076
  430.2 67.0 %all-to-all-start = ((f32[8,1,131072]{2,1,0:T(1,128)}), f32[8,1,131072]{2,1,0:T(1,128)}, u32[]{:S(2)}, u32[]{:S(2)}) async-start(f32[8,1,131072]{2,1,0:T(1,128)} %reshape.17), calls=%async_computation | async-start | bytes 8388608 | tf_op jit(solution)/shard_map/all_to_all | solution.py:80
  538.3 5.8 copy-start.3
  549.1 2.8 copy-start.1
  627.0 21.8 %slice-start = ((s8[16777216]{0:T(1024)(128)(4,1)}), s8[4194304]{0:T(1024)(128)(4,1)S(1)}, s32[]{:S(2)}) async-start(s8[16777216]{0:T(1024)(128)(4,1)} %bitcast.140), calls=%async_computation.4 | async-start | bytes 8388608
  627.0 21.8 %slice-start.1 = ((s8[16777216]{0:T(1024)(128)(4,1)}), s8[4194304]{0:T(1024)(128)(4,1)S(1)}, s32[]{:S(2)}) async-start(s8[16777216]{0:T(1024)(128)(4,1)} %bitcast.140), calls=%async_computation.5 | async-start | bytes 8388608
  634.3 7.3 %copy-start.2 = (f32[32,16,2,1024]{3,0,1,2:T(8,128)S(1)}, f32[32,16,2,1024]{3,0,1,2:T(8,128)}, u32[]{:S(2)}) copy-start(f32[32,16,2,1024]{3,0,1,2:T(8,128)} %all_to_all.46) | copy-start | bytes 12582916
  634.3 14.5 %slice-start.2 = ((s8[16777216]{0:T(1024)(128)(4,1)}), s8[4194304]{0:T(1024)(128)(4,1)S(1)}, s32[]{:S(2)}) async-start(s8[16777216]{0:T(1024)(128)(4,1)} %bitcast.140), calls=%async_computation.6 | async-start | bytes 8388608
  641.6 7.2 %slice-start.3 = ((s8[16777216]{0:T(1024)(128)(4,1)}), s8[4194304]{0:T(1024)(128)(4,1)S(1)}, s32[]{:S(2)}) async-start(s8[16777216]{0:T(1024)(128)(4,1)} %bitcast.140), calls=%async_computation.7 | async-start | bytes 8388608
  648.8 9.2 %copy-start.6 = (s32[4,128]{1,0:T(4,128)S(1)}, s32[4,128]{1,0:T(4,128)}, u32[]{:S(2)}) copy-start(s32[4,128]{1,0:T(4,128)} %param.9) | copy-start | bytes 6148
  653.3 16.6 %copy-start.5 = (f32[256,4,128]{2,1,0:T(4,128)S(1)}, f32[256,4,128]{2,1,0:T(4,128)}, u32[]{:S(2)}) copy-start(f32[256,4,128]{2,1,0:T(4,128)} %param.7) | copy-start | bytes 1572868
  654.5 14.4 %all-to-all-start.2 = ((f32[32,16,2,128]{3,1,2,0:T(8,128)}), f32[32,16,2,128]{3,1,2,0:T(8,128)S(1)}, u32[]{:S(2)}, u32[]{:S(2)}) async-start(f32[32,16,2,128]{3,1,2,0:T(8,128)} %copy.57), calls=%async_computation.2 | async-start | bytes 1048576 | tf_op jit(solution)/shard_map/all_to_all | solution.py:87
Sparse Core Ops, SparseCore 0:
  49.0 331.0 all-gather.3
